TPU v7x, 256 devices: a whole 4x4x8 slice. The times are simulated.
256 devices in a mesh: row: 8 (over y, core), col: 32 (over z, x).
Axes of the slice: x: 4, y: 4, z: 8, core: 2. Of those that a mesh axis runs over, the one named last changes fastest.
Arguments:
- right_side: bfloat16 [8, 32, 256, 512], P(None, 'col'), may hold values from -6 to 6
- inverses: bfloat16 [8, 32, 256, 256], P(None, 'col'), may hold values from -0.375 to 0.375
- factor_blocks: bfloat16 [224, 32, 2, 256, 256], P('row', 'col'), may hold values from -0.03125 to 0.03125
- pattern: int32 [224, 32, 2], P('row', 'col'), may hold values from 0 to 3, as said below
Outputs:
- solution: bfloat16 [8, 32, 256, 512], P(None, 'col')
Inputs may be any that keep to these rules, and one draw needn't show every extreme that they name: The 2 entries of one slot list of pattern name different solved blocks.
All inputs are finite; a program needn't handle non-finite values.
Results may differ from a plain program's by a relative error of at most 0.022.
Values may be sent and summed in bfloat16 or wider, within the bound.
No kernel may reach another device: no remote copies, remote signals or barrier semaphores. Data moves between devices by JAX's collectives and lax.ppermute only.
A program may use at most 128 MiB of HBM per device.

v0:
```python
import jax
import jax.numpy as jnp
from jax import lax
from jax.sharding import PartitionSpec as P

LEVELS = 8


def from_root(value, axis, source):
    kept = jnp.where(lax.axis_index(axis) == source, value, 0).astype(value.dtype)
    return lax.psum(kept, axis)


def contribution(blocks, indices, sources):
    picked = jnp.take(sources, indices, axis=0)
    return jnp.einsum("tkab,tkbn->tan", blocks, picked, preferred_element_type=jnp.float32)


def solve_blocks(inverse_level, totals):
    scaled = totals.astype(jnp.bfloat16)
    return jnp.einsum(
        "tab,tbn->tan", inverse_level, scaled, preferred_element_type=jnp.float32
    ).astype(jnp.bfloat16)


def reduce_solve(partial_value, right_level, inverse_level):
    summed = lax.psum(partial_value.astype(jnp.bfloat16), "row").astype(jnp.float32)
    return solve_blocks(inverse_level, right_level.astype(jnp.float32) - summed)


def spread_sources(solved):
    row_index = lax.axis_index("row")
    row_count = lax.axis_size("row")
    group_count = lax.axis_size("col") // row_count
    pieces = []
    for member in range(group_count):
        pieces.append(from_root(solved, "col", row_index + row_count * member))
    return jnp.concatenate(pieces, axis=0)


def shards(right_side, inverses, factor_blocks, pattern):
    solutions = []
    received = []
    for current in range(LEVELS):
        if current == 0:
            solved = solve_blocks(inverses[0], right_side[0].astype(jnp.float32))
        else:
            partial_value = None
            for earlier in range(current):
                pair_index = current * (current - 1) // 2 + earlier
                term = contribution(
                    factor_blocks[pair_index], pattern[pair_index], received[earlier]
                )
                partial_value = term if partial_value is None else partial_value + term
            solved = reduce_solve(partial_value, right_side[current], inverses[current])
        solutions.append(solved)
        if current + 1 < LEVELS:
            sources = spread_sources(solved)
            received.append(sources)
    return jnp.stack(solutions)


def solution(mesh):
    in_specs = (
        P(None, "col", None, None),
        P(None, "col", None, None),
        P("row", "col", None, None, None),
        P("row", "col", None),
    )
    out_specs = P(None, "col", None, None)
    return jax.shard_map(shards, mesh=mesh, in_specs=in_specs, out_specs=out_specs, check_vma=False)
```

profile of v0, /device:TPU:2, one launch (start us, length us, event | category | flops | bytes accessed | tf_op | source)
XLA Modules:
  0.0 1600.2 jit_solution(14815929831289566410)
XLA Ops:
  10.9 2.5 fusion.303
  21.0 141.9 %all-reduce.48.cloned.1.call-done = (bf16[1,256,512]{2,1,0:T(8,128)(2,1)}, bf16[1,256,512]{2,1,0:T(8,128)(2,1)}, bf16[1,256,512]{2,1,0:T(8,128)(2,1)}, bf16[1,256,512]{2,1,0:T(8,128)(2,1)}) async-done(((bf16[1,256,512]{2,1,0:T(8,128)(2,1)}, bf16[1,256,512]{2,1,0:T(8,128)(2,1)}, bf16[1,256,512]{2,1,0:T(8,128)(2,1)}, bf16[1,256,512]{2,1,0:T(8,128)(2,1)}), (bf16[1,256,512]{2,1,0:T(8,128)(2,1)}, ...) | async-done | bytes 1048592 | tf_op jit(solution)/shard_map/psum | solution.py:11
  169.6 63.4 %all-reduce.22.cloned.1.call-done = bf16[1,256,512]{1,2,0:T(8,128)(2,1)} async-done(((bf16[1,256,512]{1,2,0:T(8,128)(2,1)}), bf16[1,256,512]{1,2,0:T(8,128)(2,1)}) %all-reduce.22.cloned.1.call-update) | async-done | bytes 262160 | tf_op jit(solution)/shard_map/psum | solution.py:27
  236.7 148.6 %all-reduce.46.cloned.1.call-done = (bf16[1,256,512]{2,1,0:T(8,128)(2,1)}, bf16[1,256,512]{2,1,0:T(8,128)(2,1)}, bf16[1,256,512]{2,1,0:T(8,128)(2,1)}, bf16[1,256,512]{2,1,0:T(8,128)(2,1)}) async-done(((bf16[1,256,512]{2,1,0:T(8,128)(2,1)}, bf16[1,256,512]{2,1,0:T(8,128)(2,1)}, bf16[1,256,512]{2,1,0:T(8,128)(2,1)}, bf16[1,256,512]{2,1,0:T(8,128)(2,1)}), (bf16[1,256,512]{2,1,0:T(8,128)(2,1)}, ...) | async-done | bytes 1048592 | tf_op jit(solution)/shard_map/psum | solution.py:11
  394.4 63.3 %all-reduce.24.cloned.1.call-done = bf16[1,256,512]{1,2,0:T(8,128)(2,1)} async-done(((bf16[1,256,512]{1,2,0:T(8,128)(2,1)}), bf16[1,256,512]{1,2,0:T(8,128)(2,1)}) %all-reduce.24.cloned.1.call-update) | async-done | bytes 262160 | tf_op jit(solution)/shard_map/psum | solution.py:27
  466.6 142.8 %all-reduce.44.cloned.1.call-done = (bf16[1,256,512]{2,1,0:T(8,128)(2,1)}, bf16[1,256,512]{2,1,0:T(8,128)(2,1)}, bf16[1,256,512]{2,1,0:T(8,128)(2,1)}, bf16[1,256,512]{2,1,0:T(8,128)(2,1)}) async-done(((bf16[1,256,512]{2,1,0:T(8,128)(2,1)}, bf16[1,256,512]{2,1,0:T(8,128)(2,1)}, bf16[1,256,512]{2,1,0:T(8,128)(2,1)}, bf16[1,256,512]{2,1,0:T(8,128)(2,1)}), (bf16[1,256,512]{2,1,0:T(8,128)(2,1)}, ...) | async-done | bytes 1048592 | tf_op jit(solution)/shard_map/psum | solution.py:11
  621.8 60.3 %all-reduce.26.cloned.1.call-done = bf16[1,256,512]{1,2,0:T(8,128)(2,1)} async-done(((bf16[1,256,512]{1,2,0:T(8,128)(2,1)}), bf16[1,256,512]{1,2,0:T(8,128)(2,1)}) %all-reduce.26.cloned.1.call-update) | async-done | bytes 262160 | tf_op jit(solution)/shard_map/psum | solution.py:27
  695.2 139.2 %all-reduce.42.cloned.1.call-done = (bf16[1,256,512]{2,1,0:T(8,128)(2,1)}, bf16[1,256,512]{2,1,0:T(8,128)(2,1)}, bf16[1,256,512]{2,1,0:T(8,128)(2,1)}, bf16[1,256,512]{2,1,0:T(8,128)(2,1)}) async-done(((bf16[1,256,512]{2,1,0:T(8,128)(2,1)}, bf16[1,256,512]{2,1,0:T(8,128)(2,1)}, bf16[1,256,512]{2,1,0:T(8,128)(2,1)}, bf16[1,256,512]{2,1,0:T(8,128)(2,1)}), (bf16[1,256,512]{2,1,0:T(8,128)(2,1)}, ...) | async-done | bytes 1048592 | tf_op jit(solution)/shard_map/psum | solution.py:11
  841.1 2.6 gather_fusion.9
  845.2 2.6 fusion.32
  849.7 61.6 %all-reduce.28.cloned.1.call-done = bf16[1,256,512]{1,2,0:T(8,128)(2,1)} async-done(((bf16[1,256,512]{1,2,0:T(8,128)(2,1)}), bf16[1,256,512]{1,2,0:T(8,128)(2,1)}) %all-reduce.28.cloned.1.call-update) | async-done | bytes 262160 | tf_op jit(solution)/shard_map/psum | solution.py:27
  923.3 2.6 gather_fusion.13
  928.3 134.8 %all-reduce.40.cloned.1.call-done = (bf16[1,256,512]{2,1,0:T(8,128)(2,1)}, bf16[1,256,512]{2,1,0:T(8,128)(2,1)}, bf16[1,256,512]{2,1,0:T(8,128)(2,1)}, bf16[1,256,512]{2,1,0:T(8,128)(2,1)}) async-done(((bf16[1,256,512]{2,1,0:T(8,128)(2,1)}, bf16[1,256,512]{2,1,0:T(8,128)(2,1)}, bf16[1,256,512]{2,1,0:T(8,128)(2,1)}, bf16[1,256,512]{2,1,0:T(8,128)(2,1)}), (bf16[1,256,512]{2,1,0:T(8,128)(2,1)}, ...) | async-done | bytes 1048592 | tf_op jit(solution)/shard_map/psum | solution.py:11
  1069.8 2.6 gather_fusion.14
  1074.0 2.7 fusion.28
  1078.6 61.6 %all-reduce.30.cloned.1.call-done = bf16[1,256,512]{1,2,0:T(8,128)(2,1)} async-done(((bf16[1,256,512]{1,2,0:T(8,128)(2,1)}), bf16[1,256,512]{1,2,0:T(8,128)(2,1)}) %all-reduce.30.cloned.1.call-update) | async-done | bytes 262160 | tf_op jit(solution)/shard_map/psum | solution.py:27
  1152.4 2.6 gather_fusion.18
  1157.3 2.6 gather_fusion.19
  1162.3 130.3 %all-reduce.38.cloned.1.call-done = (bf16[1,256,512]{2,1,0:T(8,128)(2,1)}, bf16[1,256,512]{2,1,0:T(8,128)(2,1)}, bf16[1,256,512]{2,1,0:T(8,128)(2,1)}, bf16[1,256,512]{2,1,0:T(8,128)(2,1)}) async-done(((bf16[1,256,512]{2,1,0:T(8,128)(2,1)}, bf16[1,256,512]{2,1,0:T(8,128)(2,1)}, bf16[1,256,512]{2,1,0:T(8,128)(2,1)}, bf16[1,256,512]{2,1,0:T(8,128)(2,1)}), (bf16[1,256,512]{2,1,0:T(8,128)(2,1)}, ...) | async-done | bytes 1048592 | tf_op jit(solution)/shard_map/psum | solution.py:11
  1299.2 2.6 gather_fusion.20
  1303.4 2.9 fusion.34
  1308.2 61.5 %all-reduce.32.cloned.1.call-done = bf16[1,256,512]{1,2,0:T(8,128)(2,1)} async-done(((bf16[1,256,512]{1,2,0:T(8,128)(2,1)}), bf16[1,256,512]{1,2,0:T(8,128)(2,1)}) %all-reduce.32.cloned.1.call-update) | async-done | bytes 262160 | tf_op jit(solution)/shard_map/psum | solution.py:27
  1389.4 132.1 %all-reduce.36.cloned.1.call-done = (bf16[1,256,512]{2,1,0:T(8,128)(2,1)}, bf16[1,256,512]{2,1,0:T(8,128)(2,1)}, bf16[1,256,512]{2,1,0:T(8,128)(2,1)}, bf16[1,256,512]{2,1,0:T(8,128)(2,1)}) async-done(((bf16[1,256,512]{2,1,0:T(8,128)(2,1)}, bf16[1,256,512]{2,1,0:T(8,128)(2,1)}, bf16[1,256,512]{2,1,0:T(8,128)(2,1)}, bf16[1,256,512]{2,1,0:T(8,128)(2,1)}), (bf16[1,256,512]{2,1,0:T(8,128)(2,1)}, ...) | async-done | bytes 1048592 | tf_op jit(solution)/shard_map/psum | solution.py:11
  1528.4 63.4 %all-reduce.34.cloned.1.call-done = bf16[1,256,512]{1,2,0:T(8,128)(2,1)} async-done(((bf16[1,256,512]{1,2,0:T(8,128)(2,1)}), bf16[1,256,512]{1,2,0:T(8,128)(2,1)}) %all-reduce.34.cloned.1.call-update) | async-done | bytes 262160 | tf_op jit(solution)/shard_map/psum | solution.py:27
  (199 shorter events, 155.2 us)
Async XLA Ops:
  6.5 156.4 %all-reduce.48.cloned.1.call-start = ((), (), s32[]{:S(2)}) async-start(), calls=%async_computation.13 | async-start | bytes 2097152 | tf_op jit(solution)/shard_map/psum | solution.py:11
  9.5 223.6 %all-reduce.22.cloned.1.call-start = ((), (), s32[]{:S(2)}) async-start(), calls=%async_computation | async-start | bytes 524288 | tf_op jit(solution)/shard_map/psum | solution.py:27
  169.6 215.8 %all-reduce.46.cloned.1.call-start = ((), (), s32[]{:S(2)}) async-start(), calls=%async_computation.12 | async-start | bytes 2097152 | tf_op jit(solution)/shard_map/psum | solution.py:11
  236.0 221.7 %all-reduce.24.cloned.1.call-start = ((), (), s32[]{:S(2)}) async-start(), calls=%async_computation.1 | async-start | bytes 524288 | tf_op jit(solution)/shard_map/psum | solution.py:27
  394.2 215.1 %all-reduce.44.cloned.1.call-start = ((), (), s32[]{:S(2)}) async-start(), calls=%async_computation.11 | async-start | bytes 2097152 | tf_op jit(solution)/shard_map/psum | solution.py:11
  460.7 221.4 %all-reduce.26.cloned.1.call-start = ((), (), s32[]{:S(2)}) async-start(), calls=%async_computation.2 | async-start | bytes 524288 | tf_op jit(solution)/shard_map/psum | solution.py:27
  618.7 215.7 %all-reduce.42.cloned.1.call-start = ((), (), s32[]{:S(2)}) async-start(), calls=%async_computation.10 | async-start | bytes 2097152 | tf_op jit(solution)/shard_map/psum | solution.py:11
  685.2 226.1 %all-reduce.28.cloned.1.call-start = ((), (), s32[]{:S(2)}) async-start(), calls=%async_computation.3 | async-start | bytes 524288 | tf_op jit(solution)/shard_map/psum | solution.py:27
  845.2 80.7 %copy-start.2 = (pred[2]{0:T(512)(128)(4,1)S(1)}, pred[2]{0:T(512)(128)(4,1)}, u32[]{:S(2)}) copy-start(pred[2]{0:T(512)(128)(4,1)} %get-tuple-element.148) | copy-start | bytes 10
  847.8 215.3 %all-reduce.40.cloned.1.call-start = ((), (), s32[]{:S(2)}) async-start(), calls=%async_computation.9 | async-start | bytes 2097152 | tf_op jit(solution)/shard_map/psum | solution.py:11
  913.4 159.1 %copy-start.1 = (pred[2]{0:T(512)(128)(4,1)S(1)}, pred[2]{0:T(512)(128)(4,1)}, u32[]{:S(2)}) copy-start(pred[2]{0:T(512)(128)(4,1)} %get-tuple-element.147) | copy-start | bytes 10
  914.4 159.6 %copy-start.3 = (pred[2]{0:T(512)(128)(4,1)S(1)}, pred[2]{0:T(512)(128)(4,1)}, u32[]{:S(2)}) copy-start(pred[2]{0:T(512)(128)(4,1)} %and_bitcast_fusion.17) | copy-start | bytes 10
  914.4 225.8 %all-reduce.30.cloned.1.call-start = ((), (), s32[]{:S(2)}) async-start(), calls=%async_computation.4 | async-start | bytes 524288 | tf_op jit(solution)/shard_map/psum | solution.py:27
  928.3 218.0 %copy-start.5 = (pred[2]{0:T(512)(128)(4,1)S(1)}, pred[2]{0:T(512)(128)(4,1)}, u32[]{:S(2)}) copy-start(pred[2]{0:T(512)(128)(4,1)} %and_bitcast_fusion.11) | copy-start | bytes 10
  1076.7 215.8 %all-reduce.38.cloned.1.call-start = ((), (), s32[]{:S(2)}) async-start(), calls=%async_computation.8 | async-start | bytes 2097152 | tf_op jit(solution)/shard_map/psum | solution.py:11
  1143.3 226.5 %all-reduce.32.cloned.1.call-start = ((), (), s32[]{:S(2)}) async-start(), calls=%async_computation.5 | async-start | bytes 524288 | tf_op jit(solution)/shard_map/psum | solution.py:27
  1144.9 158.5 %copy-start.4 = (pred[2]{0:T(512)(128)(4,1)S(1)}, pred[2]{0:T(512)(128)(4,1)}, u32[]{:S(2)}) copy-start(pred[2]{0:T(512)(128)(4,1)} %and_bitcast_fusion.12) | copy-start | bytes 10
  1306.3 215.2 %all-reduce.36.cloned.1.call-start = ((), (), s32[]{:S(2)}) async-start(), calls=%async_computation.7 | async-start | bytes 2097152 | tf_op jit(solution)/shard_map/psum | solution.py:11
  1372.9 218.9 %all-reduce.34.cloned.1.call-start = ((), (), s32[]{:S(2)}) async-start(), calls=%async_computation.6 | async-start | bytes 524288 | tf_op jit(solution)/shard_map/psum | solution.py:27
  1376.2 149.5 %copy-start = (bf16[2,256,512]{2,1,0:T(8,128)(2,1)S(1)}, bf16[2,256,512]{2,1,0:T(8,128)(2,1)}, u32[]{:S(2)}) copy-start(bf16[2,256,512]{2,1,0:T(8,128)(2,1)} %gather_fusion.21) | copy-start | bytes 1572868
Sparse Core Ops, SparseCore 0:
  11.2 151.7 all-reduce.47
  169.7 63.3 all-reduce.21
  237.4 147.8 all-reduce.45
  394.3 63.3 all-reduce.23
  461.4 147.8 all-reduce.43
  618.8 63.3 all-reduce.25
  686.5 147.8 all-reduce.41
  848.0 63.3 all-reduce.27
  915.2 147.9 all-reduce.39
  1076.9 63.3 all-reduce.29
  1144.6 147.9 all-reduce.37
  1306.5 63.2 all-reduce.31
  1373.6 147.8 all-reduce.35
  1528.4 63.3 all-reduce.33
where the time goes:
time: 1600 us
  waiting for transfers between devices  1410 us (88%)
  local copies, waits for them, and re-layouts  88.4 us (6%)
  matrix products  74.1 us (5%)
  other arithmetic  18.1 us (1%)
    psum x7, waiting for transfers between devices, from_root(): return lax.psum(kept, axis)  970 us
    psum x7, waiting for transfers between devices, reduce_solve(): lax.psum(partial_value.astype(jnp.bfloat16), 'row').astype(jnp.float32)  435 us
    dot_general x28, matrix products, contribution(): jnp.einsum('tkab,tkbn->tan', blocks, picked, preferred_element_type=jnp.f...  58.2 us
    gather x28, local copies, waits for them, and re-layouts, contribution(): picked = jnp.take(sources, indices, axis=0)  43.3 us
  transfers between devices with their start and end apart: 14, of which 14 were waited for; matrix products, arithmetic and copies ran while one was open for 5% of the time, Pallas kernels for 0%

commit v1 on v0

--- a/solution.py
+++ b/solution.py
@@ -24,7 +24,9 @@
 
 
 def reduce_solve(partial_value, right_level, inverse_level):
-    summed = lax.psum(partial_value.astype(jnp.bfloat16), "row").astype(jnp.float32)
+    summed = jnp.sum(lax.all_gather(partial_value.astype(jnp.bfloat16), "row"), axis=0).astype(
+        jnp.float32
+    )
     return solve_blocks(inverse_level, right_level.astype(jnp.float32) - summed)
 
 

time: 1600 us -> 1390 us (0.87)
  waiting for transfers between devices: 1410 us -> 1170 us
    psum x7 -> x0, waiting for transfers between devices: 435 us -> none  [reduce_solve(): lax.psum(partial_value.astype(jnp.bfloat16), 'row').astype(jnp.float32)]
    all_gather x0 -> x7, waiting for transfers between devices: none -> 187 us  [reduce_solve(): lax.all_gather(partial_value.astype(jnp.bfloat16), 'row')]
    psum x7, waiting for transfers between devices: 970 us -> 988 us  [from_root(): return lax.psum(kept, axis)]
    unnamed x37 -> x40, local copies, waits for them, and re-layouts: 31.4 us -> 48.2 us
where the time goes in v1:
time: 1390 us
  waiting for transfers between devices  1170 us (84%)
  local copies, waits for them, and re-layouts  103 us (7%)
  matrix products  74.1 us (5%)
  other arithmetic  19.6 us (1%)
  between operations  14.1 us (1%)
    psum x7, waiting for transfers between devices, from_root(): return lax.psum(kept, axis)  988 us
    all_gather x7, waiting for transfers between devices, reduce_solve(): lax.all_gather(partial_value.astype(jnp.bfloat16), 'row')  187 us
    dot_general x28, matrix products, contribution(): jnp.einsum('tkab,tkbn->tan', blocks, picked, preferred_element_type=jnp.f...  58.5 us
    unnamed x40, local copies, waits for them, and re-layouts  48.2 us
    gather x28, local copies, waits for them, and re-layouts, contribution(): picked = jnp.take(sources, indices, axis=0)  44.1 us
  transfers between devices with their start and end apart: 14, of which 14 were waited for; matrix products, arithmetic and copies ran while one was open for 5% of the time, Pallas kernels for 0%

profile of v1, /device:TPU:2, one launch (start us, length us, event | category | flops | bytes accessed | tf_op | source)
XLA Modules:
  0.0 1387.1 jit_solution(10423021335103902982)
XLA Ops:
  11.1 151.9 %all-reduce.27.cloned.1.call-done = (bf16[1,256,512]{2,1,0:T(8,128)(2,1)}, bf16[1,256,512]{2,1,0:T(8,128)(2,1)}, bf16[1,256,512]{2,1,0:T(8,128)(2,1)}, bf16[1,256,512]{2,1,0:T(8,128)(2,1)}) async-done(((bf16[1,256,512]{2,1,0:T(8,128)(2,1)}, bf16[1,256,512]{2,1,0:T(8,128)(2,1)}, bf16[1,256,512]{2,1,0:T(8,128)(2,1)}, bf16[1,256,512]{2,1,0:T(8,128)(2,1)}), (bf16[1,256,512]{2,1,0:T(8,128)(2,1)}, ...) | async-done | bytes 1048592 | tf_op jit(solution)/shard_map/psum | solution.py:11
  172.9 26.0 %all-gather.15.cloned.1.call-done = bf16[2048,512]{0,1:T(8,128)(2,1)} async-done(((bf16[256,512]{0,1:T(8,128)(2,1)}), bf16[2048,512]{0,1:T(8,128)(2,1)}) %all-gather.15.cloned.1.call-update) | async-done | bytes 2097168 | tf_op jit(solution)/shard_map/all_gather | solution.py:27
  206.3 149.2 %all-reduce.25.cloned.1.call-done = (bf16[1,256,512]{2,1,0:T(8,128)(2,1)}, bf16[1,256,512]{2,1,0:T(8,128)(2,1)}, bf16[1,256,512]{2,1,0:T(8,128)(2,1)}, bf16[1,256,512]{2,1,0:T(8,128)(2,1)}) async-done(((bf16[1,256,512]{2,1,0:T(8,128)(2,1)}, bf16[1,256,512]{2,1,0:T(8,128)(2,1)}, bf16[1,256,512]{2,1,0:T(8,128)(2,1)}, bf16[1,256,512]{2,1,0:T(8,128)(2,1)}), (bf16[1,256,512]{2,1,0:T(8,128)(2,1)}, ...) | async-done | bytes 1048592 | tf_op jit(solution)/shard_map/psum | solution.py:11
  364.6 28.1 %all-gather.17.cloned.1.call-done = bf16[2048,512]{0,1:T(8,128)(2,1)} async-done(((bf16[256,512]{0,1:T(8,128)(2,1)}), bf16[2048,512]{0,1:T(8,128)(2,1)}) %all-gather.17.cloned.1.call-update) | async-done | bytes 2097168 | tf_op jit(solution)/shard_map/all_gather | solution.py:27
  403.8 145.7 %all-reduce.23.cloned.1.call-done = (bf16[1,256,512]{2,1,0:T(8,128)(2,1)}, bf16[1,256,512]{2,1,0:T(8,128)(2,1)}, bf16[1,256,512]{2,1,0:T(8,128)(2,1)}, bf16[1,256,512]{2,1,0:T(8,128)(2,1)}) async-done(((bf16[1,256,512]{2,1,0:T(8,128)(2,1)}, bf16[1,256,512]{2,1,0:T(8,128)(2,1)}, bf16[1,256,512]{2,1,0:T(8,128)(2,1)}, bf16[1,256,512]{2,1,0:T(8,128)(2,1)}), (bf16[1,256,512]{2,1,0:T(8,128)(2,1)}, ...) | async-done | bytes 1048592 | tf_op jit(solution)/shard_map/psum | solution.py:11
  561.4 25.7 %all-gather.19.cloned.1.call-done = bf16[2048,512]{0,1:T(8,128)(2,1)} async-done(((bf16[256,512]{0,1:T(8,128)(2,1)}), bf16[2048,512]{0,1:T(8,128)(2,1)}) %all-gather.19.cloned.1.call-update) | async-done | bytes 2097168 | tf_op jit(solution)/shard_map/all_gather | solution.py:27
  602.8 140.9 %all-reduce.21.cloned.1.call-done = (bf16[1,256,512]{2,1,0:T(8,128)(2,1)}, bf16[1,256,512]{2,1,0:T(8,128)(2,1)}, bf16[1,256,512]{2,1,0:T(8,128)(2,1)}, bf16[1,256,512]{2,1,0:T(8,128)(2,1)}) async-done(((bf16[1,256,512]{2,1,0:T(8,128)(2,1)}, bf16[1,256,512]{2,1,0:T(8,128)(2,1)}, bf16[1,256,512]{2,1,0:T(8,128)(2,1)}, bf16[1,256,512]{2,1,0:T(8,128)(2,1)}), (bf16[1,256,512]{2,1,0:T(8,128)(2,1)}, ...) | async-done | bytes 1048592 | tf_op jit(solution)/shard_map/psum | solution.py:11
  750.5 2.6 gather_fusion.9
  754.6 2.6 fusion.32
  759.1 26.5 %all-gather.21.cloned.1.call-done = bf16[2048,512]{0,1:T(8,128)(2,1)} async-done(((bf16[256,512]{0,1:T(8,128)(2,1)}), bf16[2048,512]{0,1:T(8,128)(2,1)}) %all-gather.21.cloned.1.call-update) | async-done | bytes 2097168 | tf_op jit(solution)/shard_map/all_gather | solution.py:27
  801.4 2.6 gather_fusion.13
  806.4 136.0 %all-reduce.19.cloned.1.call-done = (bf16[1,256,512]{2,1,0:T(8,128)(2,1)}, bf16[1,256,512]{2,1,0:T(8,128)(2,1)}, bf16[1,256,512]{2,1,0:T(8,128)(2,1)}, bf16[1,256,512]{2,1,0:T(8,128)(2,1)}) async-done(((bf16[1,256,512]{2,1,0:T(8,128)(2,1)}, bf16[1,256,512]{2,1,0:T(8,128)(2,1)}, bf16[1,256,512]{2,1,0:T(8,128)(2,1)}, bf16[1,256,512]{2,1,0:T(8,128)(2,1)}), (bf16[1,256,512]{2,1,0:T(8,128)(2,1)}, ...) | async-done | bytes 1048592 | tf_op jit(solution)/shard_map/psum | solution.py:11
  949.0 2.6 gather_fusion.14
  953.2 2.7 fusion.28
  958.2 26.0 %all-gather.23.cloned.1.call-done = bf16[2048,512]{0,1:T(8,128)(2,1)} async-done(((bf16[256,512]{0,1:T(8,128)(2,1)}), bf16[2048,512]{0,1:T(8,128)(2,1)}) %all-gather.23.cloned.1.call-update) | async-done | bytes 2097168 | tf_op jit(solution)/shard_map/all_gather | solution.py:27
  1000.0 2.6 gather_fusion.18
  1005.0 2.6 gather_fusion.19
  1009.9 131.0 %all-reduce.17.cloned.1.call-done = (bf16[1,256,512]{2,1,0:T(8,128)(2,1)}, bf16[1,256,512]{2,1,0:T(8,128)(2,1)}, bf16[1,256,512]{2,1,0:T(8,128)(2,1)}, bf16[1,256,512]{2,1,0:T(8,128)(2,1)}) async-done(((bf16[1,256,512]{2,1,0:T(8,128)(2,1)}, bf16[1,256,512]{2,1,0:T(8,128)(2,1)}, bf16[1,256,512]{2,1,0:T(8,128)(2,1)}, bf16[1,256,512]{2,1,0:T(8,128)(2,1)}), (bf16[1,256,512]{2,1,0:T(8,128)(2,1)}, ...) | async-done | bytes 1048592 | tf_op jit(solution)/shard_map/psum | solution.py:11
  1147.6 2.6 gather_fusion.20
  1151.8 2.9 fusion.34
  1156.6 26.4 %all-gather.25.cloned.1.call-done = bf16[2048,512]{0,1:T(8,128)(2,1)} async-done(((bf16[256,512]{0,1:T(8,128)(2,1)}), bf16[2048,512]{0,1:T(8,128)(2,1)}) %all-gather.25.cloned.1.call-update) | async-done | bytes 2097168 | tf_op jit(solution)/shard_map/all_gather | solution.py:27
  1206.7 133.1 %all-reduce.15.cloned.1.call-done = (bf16[1,256,512]{2,1,0:T(8,128)(2,1)}, bf16[1,256,512]{2,1,0:T(8,128)(2,1)}, bf16[1,256,512]{2,1,0:T(8,128)(2,1)}, bf16[1,256,512]{2,1,0:T(8,128)(2,1)}) async-done(((bf16[1,256,512]{2,1,0:T(8,128)(2,1)}, bf16[1,256,512]{2,1,0:T(8,128)(2,1)}, bf16[1,256,512]{2,1,0:T(8,128)(2,1)}, bf16[1,256,512]{2,1,0:T(8,128)(2,1)}), (bf16[1,256,512]{2,1,0:T(8,128)(2,1)}, ...) | async-done | bytes 1048592 | tf_op jit(solution)/shard_map/psum | solution.py:11
  1344.1 2.5 fusion.36
  1346.7 28.2 %all-gather.27.cloned.1.call-done = bf16[2048,512]{0,1:T(8,128)(2,1)} async-done(((bf16[256,512]{0,1:T(8,128)(2,1)}), bf16[2048,512]{0,1:T(8,128)(2,1)}) %all-gather.27.cloned.1.call-update) | async-done | bytes 2097168 | tf_op jit(solution)/shard_map/all_gather | solution.py:27
  (209 shorter events, 172.1 us)
Async XLA Ops:
  6.5 164.0 %copy-start = (bf16[8,1,256,512]{3,2,1,0:T(8,128)(2,1)S(1)}, bf16[8,1,256,512]{3,2,1,0:T(8,128)(2,1)}, u32[]{:S(2)}) copy-start(bf16[8,1,256,512]{3,2,1,0:T(8,128)(2,1)} %param.6) | copy-start | bytes 6291460
  6.5 156.5 %all-reduce.27.cloned.1.call-start = ((), (), s32[]{:S(2)}) async-start(), calls=%async_computation.13 | async-start | bytes 2097152 | tf_op jit(solution)/shard_map/psum | solution.py:11
  9.7 189.2 %all-gather.15.cloned.1.call-start = ((), (), s32[]{:S(2)}) async-start(), calls=%async_computation | async-start | bytes 2359296 | tf_op jit(solution)/shard_map/all_gather | solution.py:27
  170.5 185.0 %all-reduce.25.cloned.1.call-start = ((), (), s32[]{:S(2)}) async-start(), calls=%async_computation.12 | async-start | bytes 2097152 | tf_op jit(solution)/shard_map/psum | solution.py:11
  201.1 163.3 %copy-start.2 = (bf16[1,1,256,512]{3,2,1,0:T(8,128)(2,1)S(1)}, bf16[1,1,256,512]{3,2,1,0:T(8,128)(2,1)}, u32[]{:S(2)}) copy-start(bf16[1,1,256,512]{3,2,1,0:T(8,128)(2,1)} %get-tuple-element.67) | copy-start | bytes 786436
  205.6 187.1 %all-gather.17.cloned.1.call-start = ((), (), s32[]{:S(2)}) async-start(), calls=%async_computation.1 | async-start | bytes 2359296 | tf_op jit(solution)/shard_map/all_gather | solution.py:27
  364.4 185.0 %all-reduce.23.cloned.1.call-start = ((), (), s32[]{:S(2)}) async-start(), calls=%async_computation.11 | async-start | bytes 2097152 | tf_op jit(solution)/shard_map/psum | solution.py:11
  396.6 164.2 %copy-start.3 = (s32[28,1,2]{0,2,1:T(2,128)S(1)}, s32[28,1,2]{0,2,1:T(2,128)}, u32[]{:S(2)}) copy-start(s32[28,1,2]{0,2,1:T(2,128)} %param.9) | copy-start | bytes 676
  399.5 187.5 %all-gather.19.cloned.1.call-start = ((), (), s32[]{:S(2)}) async-start(), calls=%async_computation.2 | async-start | bytes 2359296 | tf_op jit(solution)/shard_map/all_gather | solution.py:27
  558.7 185.1 %all-reduce.21.cloned.1.call-start = ((), (), s32[]{:S(2)}) async-start(), calls=%async_computation.10 | async-start | bytes 2097152 | tf_op jit(solution)/shard_map/psum | solution.py:11
  593.9 191.7 %all-gather.21.cloned.1.call-start = ((), (), s32[]{:S(2)}) async-start(), calls=%async_computation.3 | async-start | bytes 2359296 | tf_op jit(solution)/shard_map/all_gather | solution.py:27
  757.3 185.1 %all-reduce.19.cloned.1.call-start = ((), (), s32[]{:S(2)}) async-start(), calls=%async_computation.9 | async-start | bytes 2097152 | tf_op jit(solution)/shard_map/psum | solution.py:11
  792.4 191.8 %all-gather.23.cloned.1.call-start = ((), (), s32[]{:S(2)}) async-start(), calls=%async_computation.4 | async-start | bytes 2359296 | tf_op jit(solution)/shard_map/all_gather | solution.py:27
  955.9 185.0 %all-reduce.17.cloned.1.call-start = ((), (), s32[]{:S(2)}) async-start(), calls=%async_computation.8 | async-start | bytes 2097152 | tf_op jit(solution)/shard_map/psum | solution.py:11
  991.1 192.0 %all-gather.25.cloned.1.call-start = ((), (), s32[]{:S(2)}) async-start(), calls=%async_computation.5 | async-start | bytes 2359296 | tf_op jit(solution)/shard_map/all_gather | solution.py:27
  1154.7 185.1 %all-reduce.15.cloned.1.call-start = ((), (), s32[]{:S(2)}) async-start(), calls=%async_computation.7 | async-start | bytes 2097152 | tf_op jit(solution)/shard_map/psum | solution.py:11
  1189.9 185.0 %all-gather.27.cloned.1.call-start = ((), (), s32[]{:S(2)}) async-start(), calls=%async_computation.6 | async-start | bytes 2359296 | tf_op jit(solution)/shard_map/all_gather | solution.py:27
  1193.5 150.5 %copy-start.1 = (bf16[2,256,512]{2,1,0:T(8,128)(2,1)S(1)}, bf16[2,256,512]{2,1,0:T(8,128)(2,1)}, u32[]{:S(2)}) copy-start(bf16[2,256,512]{2,1,0:T(8,128)(2,1)} %gather_fusion.21) | copy-start | bytes 1572868
Sparse Core Ops, SparseCore 0:
  11.2 151.7 all-reduce.26
  170.6 28.1 all-gather.14
  205.7 149.7 all-reduce.24
  364.5 28.1 all-gather.16
  399.6 149.7 all-reduce.22
  558.8 28.1 all-gather.18
  594.0 149.7 all-reduce.20
  757.4 28.1 all-gather.20
  792.6 149.7 all-reduce.18
  956.0 28.1 all-gather.22
  991.2 149.7 all-reduce.16
  1154.8 28.1 all-gather.24
  1190.0 149.7 all-reduce.14
  1346.7 28.1 all-gather.26
